TPU v7x, 32 devices: a whole 2x2x4 slice. The times are simulated.
32 devices in a mesh: group: 2 (over y), scen: 16 (over z, x, core).
Axes of the slice: x: 2, y: 2, z: 4, core: 2. Of those that a mesh axis runs over, the one named last changes fastest.
Arguments:
- scenario_rows: bfloat16 [32, 2048, 2048], P(('group', 'scen')), parts along dimension 0, may hold values from -1 to 1
- barrier: float32 [32, 2048], P(('group', 'scen')), parts along dimension 0, may hold values from 0.01 to 61
- blocks: int32 [32, 6], P(('group', 'scen')), parts along dimension 0, may hold values from 0 to 15, all different within a row
- link_diag: float32 [4096], P('group'), parts along dimension 0, may hold values from 0.2 to 2
Outputs:
- factor: float32 [256, 16, 1024], P('group', 'scen'), parts along dimension 0
- trailing: float32 [128, 16, 1024], P('group', 'scen'), parts along dimension 0
There are 2 independent parts, one for each index of `group`. A program takes and returns all parts, laid end to end along the dimension named above; each array names one. Nothing has to cross between parts.
Inputs may be any that keep to these rules, and one draw needn't show every extreme that they name: Each row names 6 distinct column blocks, and every block is named by some scenario.
All inputs are finite; a program needn't handle non-finite values.
Results may differ from a plain program's by a relative error of at most 0.0007.
Values sent between devices are 32-bit elements; how exact they have to be, the bound alone decides.
A program may use at most 128 MiB of HBM per device.

v0:
```python
import jax
import jax.numpy as jnp
from jax import lax
from jax.sharding import PartitionSpec as P

BW = 128


def with_diagonal(values, own_diag, count, device):
    local_rows = values.shape[0]
    target = jnp.arange(local_rows, dtype=jnp.int32) * count + device
    columns = jnp.arange(values.shape[1], dtype=jnp.int32)
    hit = columns[None, :] == target[:, None]
    return values + jnp.where(hit, own_diag[:, None], jnp.zeros_like(values))


def make_fold(lead_rows, carry, piece):
    update = jnp.einsum("rk,ink->rin", lead_rows, piece, precision=lax.Precision.HIGHEST)
    return carry - update


def shards(scenario_rows, barrier, blocks, link_diag):
    coupling = scenario_rows[0]
    weights = barrier[0]
    listed = blocks[0]
    count = lax.axis_size("scen")
    device = lax.axis_index("scen")
    depth, rows_all = coupling.shape
    panel = rows_all // 2
    half = panel // 2
    own_rows = rows_all // count
    first_rows = half // count
    tail_rows = panel // count
    column_block = jnp.arange(rows_all, dtype=jnp.int32) // BW
    keep = jnp.any(column_block[:, None] == listed[None, :], axis=1)
    masked = jnp.where(keep[None, :], coupling, jnp.zeros_like(coupling))
    weighted = (weights[:, None] * masked.astype(jnp.float32)).astype(jnp.bfloat16)
    lead_view = weighted.reshape(depth, own_rows, count)
    lead_cols = masked[:, :panel]
    tail_view = weighted[:, panel:].reshape(depth, tail_rows, count)
    tail_cols = masked[:, panel:]
    piece = lead_view
    out = jnp.einsum("kmd,kc->dmc", piece, lead_cols, preferred_element_type=jnp.float32)
    first_sum = lax.psum_scatter(
        out.reshape(lax.axis_size("scen") * own_rows, panel),
        "scen",
        scatter_dimension=0,
        tiled=True,
    )
    piece = tail_view
    out = jnp.einsum("kmd,kc->dmc", piece, tail_cols, preferred_element_type=jnp.float32)
    second_sum = lax.psum_scatter(
        out.reshape(lax.axis_size("scen") * tail_rows, panel),
        "scen",
        scatter_dimension=0,
        tiled=True,
    )
    diag_own = lax.dynamic_index_in_dim(
        link_diag.reshape(own_rows, count), device, 1, keepdims=False
    )
    first_sum = jnp.concatenate(
        [
            with_diagonal(first_sum[: 2 * first_rows], diag_own[: 2 * first_rows], count, device),
            first_sum[2 * first_rows :],
        ],
        axis=0,
    )
    second_sum = with_diagonal(second_sum, diag_own[2 * first_rows :], count, device)

    def pick(matrix):
        return lax.dynamic_index_in_dim(
            matrix.reshape(first_rows, count, half), device, 1, keepdims=False
        )

    top_block = lax.all_gather(
        first_sum[:first_rows, None, :half], "scen", axis=1, tiled=True
    ).reshape(half, half)
    low_one = jnp.linalg.cholesky(top_block)
    own_one = pick(low_one)
    rest_one = jax.scipy.linalg.solve_triangular(
        low_one, first_sum[first_rows:, :half].T, lower=True
    ).T
    middle_rows = rest_one[:first_rows]
    below, slab = (
        lax.all_gather(middle_rows[:, None, :], "scen", axis=1, tiled=True),
        lax.all_gather(
            first_sum[first_rows : 2 * first_rows, None, half:], "scen", axis=1, tiled=True
        ),
    )
    below = below.reshape(half, half)
    corner = slab.reshape(half, half) - jnp.dot(below, below.T, precision=lax.Precision.HIGHEST)
    remain = first_sum[2 * first_rows :, half:] - jnp.dot(
        rest_one[first_rows:], below.T, precision=lax.Precision.HIGHEST
    )
    low_two = jnp.linalg.cholesky(corner)
    own_two = pick(low_two)
    rest_two = jax.scipy.linalg.solve_triangular(low_two, remain.T, lower=True).T
    lower_one = rest_one[first_rows:]
    top = jnp.concatenate([own_one, jnp.zeros((first_rows, half), jnp.float32)], axis=1)
    middle = jnp.concatenate([middle_rows, own_two], axis=1)
    bottom = jnp.concatenate([lower_one, rest_two], axis=1)
    factor = jnp.concatenate([top, middle, bottom], axis=0)
    initial = second_sum.reshape(tail_rows, tail_rows, count)
    trailing = make_fold(
        bottom, initial, lax.all_gather(bottom[:, None, :], "scen", axis=1, tiled=True)
    )
    return (factor[:, None, :], trailing.reshape(tail_rows, panel)[:, None, :])


def solution(mesh):
    return jax.shard_map(
        shards,
        mesh=mesh,
        in_specs=(
            P(("group", "scen"), None, None),
            P(("group", "scen"), None),
            P(("group", "scen"), None),
            P("group"),
        ),
        out_specs=(P("group", "scen", None), P("group", "scen", None)),
        check_vma=False,
    )
```

profile of v0, /device:TPU:0, one launch (start us, length us, event | category | flops | bytes accessed | tf_op | source)
XLA Modules:
  0.0 645.3 jit_solution(9764380180728750595)
XLA Ops:
  25.6 10.9 %fusion.5 = f32[1024,64,16]{0,1,2:T(8,128)} fusion(bf16[2048,64,16]{0,2,1:T(8,128)(2,1)} %bitcast.150, bf16[2048,2048]{1,0:T(8,128)(2,1)} %bitcast_select_fusion), kind=kOutput, calls=%fused_computation.13 | convolution fusion | flops 4294967296 | bytes 12582912 | tf_op jit(solution)/shard_map/kmd,kc->dmc/dot_general | solution.py:51
  37.0 12.4 %copy.42 = bf16[1,2048,2048]{1,2,0:T(8,128)(2,1)} copy(bf16[1,2048,2048]{2,1,0:T(8,128)(2,1)} %param.5) | data formatting | bytes 16777216 | tf_op args[0]
  54.9 24.5 %fusion = f32[1024,128,16]{0,1,2:T(8,128)} fusion(bf16[2048,128,16]{0,2,1:T(8,128)(2,1)S(1)} %multiply_convert_fusion, bf16[2048,2048]{1,0:T(8,128)(2,1)} %bitcast_select_fusion), kind=kOutput, calls=%fused_computation.6 | convolution fusion | flops 8589934592 | bytes 20971520 | tf_op jit(solution)/shard_map/kmd,kc->dmc/dot_general | solution.py:43
  80.4 31.8 %reduce-scatter.5.cloned.1.call-done = f32[64,1024]{1,0:T(8,128)} async-done(((f32[1024,1024]{1,0:T(8,128)}), f32[64,1024]{1,0:T(8,128)}) %reduce-scatter.5.cloned.1.call-update) | async-done | bytes 262160 | tf_op jit(solution)/shard_map/reduce_scatter | solution.py:52
  112.2 106.6 %reduce-scatter.3.cloned.1.call-done = f32[128,1024]{1,0:T(8,128)} async-done(((f32[2048,1024]{1,0:T(8,128)}), f32[128,1024]{1,0:T(8,128)}) %reduce-scatter.3.cloned.1.call-update) | async-done | bytes 524304 | tf_op jit(solution)/shard_map/reduce_scatter | solution.py:44
  222.1 36.8 %all-gather.9.cloned.1.call-done = f32[32,8192]{1,0:T(8,128)} async-done(((f32[32,512]{1,0:T(8,128)}), f32[32,8192]{1,0:T(8,128)}) %all-gather.9.cloned.1.call-update) | async-done | bytes 1048592 | tf_op jit(solution)/shard_map/all_gather | solution.py:75
  261.0 11.7 %cholesky.286 = f32[128,128]{1,0:T(8,128)S(1)} custom-call(f32[128,128]{1,0:T(8,128)S(1)} %cholesky.426), custom_call_target="Cholesky" | custom-call | tf_op jit(solution)/shard_map/jit(cholesky)/cholesky | solution.py:78
  272.8 9.8 %custom-call.33 = f32[1,128,128]{1,2,0:T(8,128)S(1)} custom-call(f32[1,128,128]{2,1,0:T(8,128)S(1)} %get-tuple-element.76), custom_call_target="InvertDiagBlocksLowerTriangular" | custom-call | tf_op jit(solution)/shard_map/jit(cholesky)/cholesky | solution.py:78
  283.3 11.7 %cholesky.305 = f32[128,128]{1,0:T(8,128)S(1)} custom-call(f32[128,128]{1,0:T(8,128)S(1)} %cholesky.430), custom_call_target="Cholesky" | custom-call | tf_op jit(solution)/shard_map/jit(cholesky)/cholesky | solution.py:78
  295.1 10.2 %custom-call.34 = f32[1,128,128]{1,2,0:T(8,128)S(1)} custom-call(f32[1,128,128]{2,1,0:T(8,128)S(1)} %get-tuple-element.73), custom_call_target="InvertDiagBlocksLowerTriangular" | custom-call | tf_op jit(solution)/shard_map/jit(cholesky)/cholesky | solution.py:78
  306.0 11.7 %cholesky.326 = f32[128,128]{1,0:T(8,128)S(1)} custom-call(f32[128,128]{1,0:T(8,128)S(1)} %cholesky.435), custom_call_target="Cholesky" | custom-call | tf_op jit(solution)/shard_map/jit(cholesky)/cholesky | solution.py:78
  317.7 9.8 %custom-call.35 = f32[1,128,128]{1,2,0:T(8,128)S(1)} custom-call(f32[1,128,128]{2,1,0:T(8,128)S(1)} %get-tuple-element.70), custom_call_target="InvertDiagBlocksLowerTriangular" | custom-call | tf_op jit(solution)/shard_map/jit(cholesky)/cholesky | solution.py:78
  328.1 11.7 %cholesky.343 = f32[128,128]{1,0:T(8,128)S(1)} custom-call(f32[128,128]{1,0:T(8,128)S(1)} %convolution_subtract_fusion.7), custom_call_target="Cholesky" | custom-call | tf_op jit(solution)/shard_map/jit(cholesky)/cholesky | solution.py:78
  354.9 39.3 %custom-call.28 = f32[4,128,128]{1,2,0:T(8,128)S(1)} custom-call(f32[4,128,128]{2,1,0:T(8,128)S(1)} %get-tuple-element.10), custom_call_target="InvertDiagBlocksLowerTriangular" | custom-call | tf_op jit(solution)/shard_map/jit(_solve_triangular)/triangular_solve | solution.py:80
  398.5 35.1 %all-gather.13.cloned.1.call-done = f32[32,8192]{1,0:T(8,128)} async-done(((f32[32,512]{1,0:T(8,128)}), f32[32,8192]{1,0:T(8,128)}) %all-gather.13.cloned.1.call-update) | async-done | bytes 1048592 | tf_op jit(solution)/shard_map/all_gather | solution.py:85
  438.5 11.7 %cholesky.358 = f32[128,128]{1,0:T(8,128)S(1)} custom-call(f32[128,128]{1,0:T(8,128)S(1)} %cholesky.439), custom_call_target="Cholesky" | custom-call | tf_op jit(solution)/shard_map/jit(cholesky)/cholesky | solution.py:95
  450.4 9.8 %custom-call.36 = f32[1,128,128]{1,2,0:T(8,128)S(1)} custom-call(f32[1,128,128]{2,1,0:T(8,128)S(1)} %get-tuple-element.66), custom_call_target="InvertDiagBlocksLowerTriangular" | custom-call | tf_op jit(solution)/shard_map/jit(cholesky)/cholesky | solution.py:95
  462.8 12.1 %cholesky.377 = f32[128,128]{1,0:T(8,128)S(1)} custom-call(f32[128,128]{1,0:T(8,128)S(1)} %cholesky.443), custom_call_target="Cholesky" | custom-call | tf_op jit(solution)/shard_map/jit(cholesky)/cholesky | solution.py:95
  474.9 9.8 %custom-call.37 = f32[1,128,128]{1,2,0:T(8,128)S(1)} custom-call(f32[1,128,128]{2,1,0:T(8,128)S(1)} %get-tuple-element.63), custom_call_target="InvertDiagBlocksLowerTriangular" | custom-call | tf_op jit(solution)/shard_map/jit(cholesky)/cholesky | solution.py:95
  486.3 11.7 %cholesky.398 = f32[128,128]{1,0:T(8,128)S(1)} custom-call(f32[128,128]{1,0:T(8,128)S(1)} %cholesky.448), custom_call_target="Cholesky" | custom-call | tf_op jit(solution)/shard_map/jit(cholesky)/cholesky | solution.py:95
  498.0 9.8 %custom-call.38 = f32[1,128,128]{1,2,0:T(8,128)S(1)} custom-call(f32[1,128,128]{2,1,0:T(8,128)S(1)} %get-tuple-element.60), custom_call_target="InvertDiagBlocksLowerTriangular" | custom-call | tf_op jit(solution)/shard_map/jit(cholesky)/cholesky | solution.py:95
  509.3 11.9 %cholesky.415 = f32[128,128]{1,0:T(8,128)S(1)} custom-call(f32[128,128]{1,0:T(8,128)S(1)} %convolution_subtract_fusion.6), custom_call_target="Cholesky" | custom-call | tf_op jit(solution)/shard_map/jit(cholesky)/cholesky | solution.py:95
  535.8 39.3 %custom-call.29 = f32[4,128,128]{1,2,0:T(8,128)S(1)} custom-call(f32[4,128,128]{2,1,0:T(8,128)S(1)} %get-tuple-element.18), custom_call_target="InvertDiagBlocksLowerTriangular" | custom-call | tf_op jit(solution)/shard_map/jit(_solve_triangular)/triangular_solve | solution.py:97
  583.7 45.4 %all-gather.15.cloned.1.call-done = f32[64,16384]{1,0:T(8,128)} async-done(((f32[64,1024]{1,0:T(8,128)}), f32[64,16384]{1,0:T(8,128)}) %all-gather.15.cloned.1.call-update) | async-done | bytes 4194320 | tf_op jit(solution)/shard_map/all_gather | solution.py:105
  (141 shorter events, 106.1 us)
Async XLA Ops:
  7.2 105.0 %reduce-scatter.5.cloned.1.call-start = ((), (), s32[]{:S(2)}) async-start(), calls=%async_computation.3 | async-start | bytes 4456448 | tf_op jit(solution)/shard_map/reduce_scatter | solution.py:52
  8.0 7.2 %copy-start.2 = (f32[1,2048]{1,0:T(1,128)S(1)}, f32[1,2048]{1,0:T(1,128)}, u32[]{:S(2)}) copy-start(f32[1,2048]{1,0:T(1,128)} %param.6) | copy-start | bytes 24580
  36.5 182.2 %reduce-scatter.3.cloned.1.call-start = ((), (), s32[]{:S(2)}) async-start(), calls=%async_computation.2 | async-start | bytes 8912896 | tf_op jit(solution)/shard_map/reduce_scatter | solution.py:44
  79.4 0.7 copy-start.3
  79.4 179.6 %all-gather.9.cloned.1.call-start = ((), (), s32[]{:S(2)}) async-start(), calls=%async_computation.4 | async-start | bytes 1114112 | tf_op jit(solution)/shard_map/all_gather | solution.py:75
  221.3 175.4 %all-gather.11.cloned.1.call-start = ((), (), s32[]{:S(2)}) async-start(), calls=%async_computation.5 | async-start | bytes 1114112 | tf_op jit(solution)/shard_map/all_gather | solution.py:86
  221.9 211.8 %all-gather.13.cloned.1.call-start = ((), (), s32[]{:S(2)}) async-start(), calls=%async_computation.6 | async-start | bytes 1114112 | tf_op jit(solution)/shard_map/all_gather | solution.py:85
  396.7 232.4 %all-gather.15.cloned.1.call-start = ((), (), s32[]{:S(2)}) async-start(), calls=%async_computation.7 | async-start | bytes 4456448 | tf_op jit(solution)/shard_map/all_gather | solution.py:105
  437.5 1.0 copy-start
  438.5 143.8 %copy-start.1 = (f32[32,512]{1,0:T(8,128)S(1)}, f32[32,512]{1,0:T(8,128)}, u32[]{:S(2)}) copy-start(f32[32,512]{1,0:T(8,128)} %slice.206) | copy-start | bytes 196612
Sparse Core Ops, SparseCore 0:
  36.6 75.5 reduce-scatter.4
  116.2 102.4 reduce-scatter.2
  221.4 37.4 all-gather.8
  261.6 37.2 all-gather.10
  396.8 36.8 all-gather.12
  579.7 49.3 all-gather.14
where the time goes:
time: 652 us; the launch traced here: 645 us
  other arithmetic  261 us (40%)
  waiting for transfers between devices  256 us (39%)
  matrix products  57.9 us (9%)
  local copies, waits for them, and re-layouts  49.1 us (8%)
  between operations  19.9 us (3%)
    reduce_scatter x1, waiting for transfers between devices, shards(): lax.psum_scatter(out.reshape(lax.axis_size('scen') * own_rows, panel), 's...  107 us
    another operation x15, other arithmetic, shards(): low_one = jnp.linalg.cholesky(top_block)  79.7 us
    another operation x15, other arithmetic, shards(): low_two = jnp.linalg.cholesky(corner)  79.6 us
    all_gather x1, waiting for transfers between devices, shards(): lax.all_gather(bottom[:, None, :], 'scen', axis=1, tiled=True)  45.4 us
    another operation x2, other arithmetic, shards(): jax.scipy.linalg.solve_triangular(low_two, remain.T, lower=True)  40.6 us
    another operation x3, other arithmetic, shards(): jax.scipy.linalg.solve_triangular(low_one, first_sum[first_rows:, :half]....  40.6 us
    all_gather x1, waiting for transfers between devices, shards(): lax.all_gather(first_sum[:first_rows, None, :half], 'scen', axis=1, tiled...  36.8 us
    all_gather x1, waiting for transfers between devices, shards(): lax.all_gather(middle_rows[:, None, :], 'scen', axis=1, tiled=True)  35.1 us
  transfers between devices with their start and end apart: 6, of which 5 were waited for; matrix products, arithmetic and copies ran while one was open for 28% of the time, Pallas kernels for 0%

commit v1 on v0

v1 whole, which is shorter than its diff:
```python
import functools

import jax
import jax.numpy as jnp
from jax import lax
from jax.experimental import pallas as pl
from jax.experimental.pallas import tpu as pltpu
from jax.sharding import PartitionSpec as P

BW = 128
HI = lax.Precision.HIGHEST


def contract(left, right, dims):
    return lax.dot_general(left, right, (dims, ((), ())), precision=HI, preferred_element_type=jnp.float32)


def gram_kernel(listed, *refs, touched, count):
    weights = refs[touched][...]
    out = refs[touched + 1]
    whole = refs[touched + 2]
    depth = weights.shape[1]
    right = jnp.concatenate([refs[i][...] for i in range(touched)], axis=1)
    for i in range(touched):
        turned = refs[i][...].T
        left = (weights * turned.astype(jnp.float32)).astype(jnp.bfloat16)
        part = lax.dot_general(left, right, (((1,), (0,)), ((), ())), preferred_element_type=jnp.float32)
        for j in range(touched):
            whole[j, i * BW : (i + 1) * BW, :] = part[:, j * BW : (j + 1) * BW]
    for owner in range(count):
        for j in range(touched):
            out[owner, :, j * BW : (j + 1) * BW] = whole[j, pl.ds(owner, touched * BW // count, stride=count), :]


def gram(coupling, weights, listed, count):
    depth, rows_all = coupling.shape
    touched = listed.shape[0]
    specs = [
        pl.BlockSpec((depth, BW), functools.partial(lambda i, step, names: (0, names[i]), i)) for i in range(touched)
    ]
    rows = touched * BW // count
    return pl.pallas_call(
        functools.partial(gram_kernel, touched=touched, count=count),
        out_shape=jax.ShapeDtypeStruct((count, rows, touched * BW), jnp.float32),
        grid_spec=pltpu.PrefetchScalarGridSpec(
            num_scalar_prefetch=1,
            grid=(1,),
            in_specs=specs + [pl.BlockSpec((1, depth), lambda step, names: (0, 0))],
            out_specs=pl.BlockSpec((count, rows, touched * BW), lambda step, names: (0, 0, 0)),
            scratch_shapes=[pltpu.VMEM((touched, touched * BW, BW), jnp.float32)],
        ),
        compiler_params=pltpu.CompilerParams(vmem_limit_bytes=50 * 1024 * 1024),
        name="gram",
    )(listed, *([coupling] * touched), weights)


def sum_kernel(listed, device, pieces, diag, out, *, touched, count):
    groups, each, columns = out.shape
    block = lax.broadcasted_iota(jnp.int32, out.shape, 0)
    inner = lax.broadcasted_iota(jnp.int32, out.shape, 1)
    column = lax.broadcasted_iota(jnp.int32, out.shape, 2)
    row = (block * each + inner) * count + device[0]
    out[...] = jnp.where(column == row, diag[...][None], 0.0)

    def add(source, carry):
        names = [listed[source * touched + i] for i in range(touched)]
        for i in range(touched):
            for j in range(touched):
                at = pl.ds(pl.multiple_of(names[j] * BW, BW), BW)
                out[names[i], :, at] += pieces[source, i * each : (i + 1) * each, j * BW : (j + 1) * BW]
        return carry

    lax.fori_loop(0, count, add, 0)


def sum_pieces(pieces, listed, device, diag, count):
    touched = listed.shape[1]
    each = BW // count
    rows_all = diag.shape[0]
    return pl.pallas_call(
        functools.partial(sum_kernel, touched=touched, count=count),
        out_shape=jax.ShapeDtypeStruct((rows_all // BW, each, rows_all), jnp.float32),
        in_specs=[
            pl.BlockSpec(memory_space=pltpu.SMEM),
            pl.BlockSpec(memory_space=pltpu.SMEM),
            pl.BlockSpec(memory_space=pltpu.VMEM),
            pl.BlockSpec(memory_space=pltpu.VMEM),
        ],
        out_specs=pl.BlockSpec(memory_space=pltpu.VMEM),
        compiler_params=pltpu.CompilerParams(vmem_limit_bytes=50 * 1024 * 1024),
        name="sum_pieces",
    )(listed.reshape(-1), device.reshape(1), pieces, diag[None, :])


def eliminate(tile):
    tiles = BW // 8
    sub = lax.broadcasted_iota(jnp.int32, (8, BW), 0)
    lane = lax.broadcasted_iota(jnp.int32, (8, BW), 1)
    a = [tile[8 * g : 8 * g + 8, :] for g in range(tiles)]
    v = [jnp.where(lane == sub + 8 * g, 1.0, 0.0).astype(jnp.float32) for g in range(tiles)]
    for j in range(0, BW, 2):
        g0, s0 = j // 8, j % 8
        row0, row1 = a[g0][s0 : s0 + 1, :], a[g0][s0 + 1 : s0 + 2, :]
        inv0, inv1 = v[g0][s0 : s0 + 1, :], v[g0][s0 + 1 : s0 + 2, :]
        pivot = row0[:, j : j + 1]
        cross = row0[:, j + 1 : j + 2]
        other = row1[:, j + 1 : j + 2]
        recip = 1.0 / pivot
        ratio = cross * recip
        recip1 = 1.0 / (other - cross * ratio)
        next_row = row1 - ratio * row0
        next_inv = inv1 - ratio * inv0
        row0s, inv0s = row0 * recip, inv0 * recip
        row1s, inv1s = next_row * recip1, next_inv * recip1
        for g in range(g0, tiles):
            c0 = jnp.broadcast_to(a[g][:, j : j + 1], (8, BW))
            c1 = jnp.broadcast_to(a[g][:, j + 1 : j + 2], (8, BW)) - c0 * ratio
            if g == g0:
                c0 = jnp.where(sub > s0, c0, 0.0)
                c1 = jnp.where(sub > s0 + 1, c1, 0.0)
            a[g] = a[g] - c0 * row0s - c1 * row1s
            v[g] = v[g] - c0 * inv0s - c1 * inv1s
    upper, inverse = [], []
    for g in range(tiles):
        own = jnp.sum(jnp.where(lane == sub + 8 * g, a[g], 0.0), axis=1, keepdims=True)
        scale = 1.0 / jnp.sqrt(own)
        upper.append(jnp.where(lane >= sub + 8 * g, a[g] * scale, 0.0))
        inverse.append(jnp.where(lane <= sub + 8 * g, v[g] * scale, 0.0))
    return jnp.concatenate(upper, axis=0).T, jnp.concatenate(inverse, axis=0)


def factor_kernel(top, own, low, rest, solved, work, inverses):
    half = top.shape[1]
    panel = 2 * half
    steps = panel // BW
    tail = own.shape[0]
    total = panel + tail
    for at in (0, half):
        square = top[2 * at : 2 * at + half, :]
        work[at : at + half, at : at + half] = 0.5 * (square + square.T)
    work[half:panel, :half] = top[half:panel, :]
    work[:half, half:] = jnp.zeros((half, half), jnp.float32)
    work[panel:, :] = own[...]
    low[...] = jnp.zeros_like(low)

    def step(b, carry):
        place = pl.ds(pl.multiple_of(b * BW, BW), BW)
        lower, inverse = eliminate(work[place, place])
        low[place, place] = lower
        inverses[b] = inverse
        for k in range(steps):

            @pl.when(b == k)
            def _():
                lo, hi = k * BW, (k + 1) * BW
                strip = contract(work[hi:total, lo:hi], inverses[k], ((1,), (1,)))
                rest[:, lo:hi] = strip[panel - hi :]
                if hi < panel:
                    low[hi:panel, lo:hi] = strip[: panel - hi]
                    for left in range(hi, panel, BW * 2):
                        right = min(left + BW * 2, panel)
                        work[left:total, left:right] -= contract(
                            strip[left - hi :], strip[left - hi : right - hi], ((1,), (1,))
                        )

        return carry

    lax.fori_loop(0, steps, step, 0)
    for k in range(steps - 1, -1, -1):
        lo, hi = k * BW, (k + 1) * BW
        value = rest[:, lo:hi]
        if hi < panel:
            value = value - contract(solved[:, hi:panel], low[hi:panel, lo:hi], ((1,), (0,)))
        solved[:, lo:hi] = contract(value, inverses[k], ((1,), (0,)))


def factorize(top, own):
    half = top.shape[1]
    panel = 2 * half
    tail = own.shape[0]
    return pl.pallas_call(
        factor_kernel,
        out_shape=(
            jax.ShapeDtypeStruct((panel, panel), jnp.float32),
            jax.ShapeDtypeStruct((tail, panel), jnp.float32),
            jax.ShapeDtypeStruct((tail, panel), jnp.float32),
        ),
        in_specs=[pl.BlockSpec(memory_space=pltpu.VMEM)] * 2,
        out_specs=(pl.BlockSpec(memory_space=pltpu.VMEM),) * 3,
        scratch_shapes=[
            pltpu.VMEM((panel + tail, panel), jnp.float32),
            pltpu.VMEM((panel // BW, BW, BW), jnp.float32),
        ],
        compiler_params=pltpu.CompilerParams(vmem_limit_bytes=50 * 1024 * 1024),
        cost_estimate=pl.CostEstimate(flops=80_000_000_000, bytes_accessed=12_000_000, transcendentals=0),
        name="factorize",
    )(top, own)


def shards(scenario_rows, barrier, blocks, link_diag):
    coupling = scenario_rows[0]
    listed = blocks[0]
    count = lax.axis_size("scen")
    device = lax.axis_index("scen").astype(jnp.int32)
    depth, rows_all = coupling.shape
    panel = rows_all // 2
    half = panel // 2
    own_rows = rows_all // count
    first_rows = half // count
    all_listed = lax.all_gather(listed, "scen")
    pieces = gram(coupling, barrier, listed, count)
    pieces = lax.all_to_all(pieces, "scen", 0, 0)
    sums = sum_pieces(pieces, all_listed, device, link_diag, count).reshape(own_rows, rows_all)
    head = jnp.concatenate([sums[: 2 * first_rows, :half], sums[first_rows : 2 * first_rows, half:panel]], axis=0)
    tail = sums[2 * first_rows :, :panel]
    top = lax.all_gather(head[:, None, :], "scen", axis=1, tiled=True)
    tail, top = lax.optimization_barrier((tail, top))
    bottom = lax.all_gather(tail[:, None, :], "scen", axis=1, tiled=True)
    low, rest, solved = factorize(top.reshape(3 * half, half), tail)
    own_low = lax.dynamic_index_in_dim(low.reshape(2 * first_rows, count, panel), device, 1, keepdims=False)
    factor = jnp.concatenate([own_low, rest], axis=0)
    second = sums[2 * first_rows :, panel:]
    update = jnp.einsum("rk,ink->rin", solved, bottom, precision=HI)
    trailing = second - update.reshape(second.shape)
    return (factor[:, None, :], trailing[:, None, :])


def solution(mesh):
    return jax.shard_map(
        shards,
        mesh=mesh,
        in_specs=(
            P(("group", "scen"), None, None),
            P(("group", "scen"), None),
            P(("group", "scen"), None),
            P("group"),
        ),
        out_specs=(P("group", "scen", None), P("group", "scen", None)),
        check_vma=False,
    )
```

time: 652 us -> 284 us (0.44)
  other arithmetic: 261 us -> 2.46 us
  waiting for transfers between devices: 256 us -> 53.1 us
  Pallas kernels: 0 us -> 131 us
  blocking collectives: 0 us -> 54.5 us
  matrix products: 57.9 us -> 7.94 us
  local copies, waits for them, and re-layouts: 49.1 us -> 12.1 us
  starting transfers between devices: 0.89 us -> 7.59 us
    another operation x35 -> x0, other arithmetic: 240 us -> none  [the longest x15 79.7 us: shards(): low_one = jnp.linalg.cholesky(top_block)]
    reduce_scatter x2 -> x0, waiting for transfers between devices: 138 us -> none  [the longest x1 107 us: shards(): lax.psum_scatter(out.reshape(lax.axis_size('scen') * own_rows, panel), 's...]
    pallas_call x0 -> x3, Pallas kernels: none -> 131 us  [the longest x1 122 us: factorize(): pl.pallas_call(factor_kernel, out_shape=(jax.ShapeDtypeStruct((panel, pan...]
    all_gather x4 -> x2, waiting for transfers between devices: 117 us -> 53.1 us  [the longest x1 53.1 us: shards(): top = lax.all_gather(head[:, None, :], 'scen', axis=1, tiled=True)]
    all_gather x0 -> x1, blocking collectives: none -> 54.5 us  [shards(): all_listed = lax.all_gather(listed, 'scen')]
    dot_general x5 -> x1, matrix products: 47.2 us -> 7.94 us  [shards(): update = jnp.einsum('rk,ink->rin', solved, bottom, precision=HI)]
    another operation x33 -> x0, local copies, waits for them, and re-layouts: 16.6 us -> none
    another operation x26 -> x0, matrix products: 10.7 us -> none  [the longest x6 5.47 us: shards(): low_two = jnp.linalg.cholesky(corner)]
  transfers between devices with their start and end apart: 6 -> 3, of which waited for: 5 -> 1; matrix products, arithmetic and copies ran while one was open for 28% -> 2% of each run, Pallas kernels for 0% -> 43%
where the time goes in v1:
time: 284 us; the launch traced here: 283 us
  Pallas kernels  131 us (46%)
  blocking collectives  54.5 us (19%)
  waiting for transfers between devices  53.1 us (19%)
  between operations  14.2 us (5%)
  local copies, waits for them, and re-layouts  12.1 us (4%)
  matrix products  7.94 us (3%)
  starting transfers between devices  7.59 us (3%)
    pallas_call x1, Pallas kernels, factorize(): pl.pallas_call(factor_kernel, out_shape=(jax.ShapeDtypeStruct((panel, pan...  122 us
    all_gather x1, blocking collectives, shards(): all_listed = lax.all_gather(listed, 'scen')  54.5 us
    all_gather x1, waiting for transfers between devices, shards(): top = lax.all_gather(head[:, None, :], 'scen', axis=1, tiled=True)  53.1 us
    unnamed x18, local copies, waits for them, and re-layouts  8.53 us
    dot_general x1, matrix products, shards(): update = jnp.einsum('rk,ink->rin', solved, bottom, precision=HI)  7.94 us
    all_to_all x1, starting transfers between devices, shards(): pieces = lax.all_to_all(pieces, 'scen', 0, 0)  7.51 us
    pallas_call x1, Pallas kernels, gram(): pl.pallas_call(functools.partial(gram_kernel, touched=touched, count=coun...  7.22 us
  transfers between devices with their start and end apart: 3, of which 1 were waited for; matrix products, arithmetic and copies ran while one was open for 2% of the time, Pallas kernels for 43%

profile of v1, /device:TPU:0, one launch (start us, length us, event | category | flops | bytes accessed | tf_op | source)
XLA Modules:
  0.0 283.3 jit_solution(13811717429071617773)
XLA Ops:
  7.2 0.7 copy-done.3
  7.9 0.7 copy-done.5
  8.5 7.2 %gram.1 = f32[16,48,768]{2,1,0:T(8,128)} custom-call(s32[6]{0:T(128)S(1)} %bitcast.31, bf16[2048,2048]{1,0:T(8,128)(2,1)} %bitcast.33, bf16[2048,2048]{1,0:T(8,128)(2,1)} %bitcast.34, bf16[2048,2048]{1,0:T(8,128)(2,1)} %bitcast.35, bf16[2048,2048]{1,0:T(8,128)(2,1)} %bitcast.36, bf16[2048,2048]{1,0:T(8,128)(2,1)} %bitcast.37, bf16[2048,2048]{1,0:T(8,128)(2,1)} %bitcast.38, ...), custom_call_target="tpu_custom_call" | custom-call | tf_op jit(solution)/shard_map/gram/pallas_call | solution.py:42
  15.7 7.5 %all-to-all-start = ((f32[16,48,768]{2,1,0:T(8,128)}), f32[16,48,768]{2,1,0:T(8,128)S(1)}, u32[]{:S(2)}, u32[]{:S(2)}) async-start(f32[16,48,768]{2,1,0:T(8,128)} %gram.1), calls=%async_computation | async-start | bytes 4718592 | tf_op jit(solution)/shard_map/all_to_all | solution.py:212
  23.3 0.0 all-gather.6.cloned.1.call-start
  23.3 54.5 %all-gather.2 = s32[16,1,6]{2,1,0:T(1,128)S(1)} all-gather(s32[1,1,6]{2,1,0:T(1,128)S(1)} %bitcast.32), channel_id=1, replica_groups=mesh['group'=2,'scen'=16] {'scen'}, dimensions={0}, use_global_device_ids=true | all-gather | bytes 408 | tf_op jit(solution)/shard_map/all_gather | solution.py:210
  77.8 0.5 broadcast.3
  78.3 0.7 reduce.3
  79.0 0.1 reshape.22.listed
  79.1 2.1 sum_pieces.1
  81.3 0.8 pad_maximum_fusion
  82.0 0.0 all-gather.8.cloned.1.call-start
  82.1 0.7 slice.16.own
  82.8 53.1 %all-gather.6.cloned.1.call-done = f32[96,8192]{1,0:T(8,128)} async-done(((f32[96,512]{1,0:T(8,128)}), f32[96,8192]{1,0:T(8,128)}) %all-gather.6.cloned.1.call-update) | async-done | bytes 3145744 | tf_op jit(solution)/shard_map/all_gather | solution.py:216
  135.9 4.1 %copy.25 = f32[12,8,16,512]{3,2,1,0:T(8,128)S(1)} copy(f32[12,8,16,512]{3,1,2,0:T(8,128)} %bitcast.40) | data formatting | bytes 6291456
  140.1 122.1 %factorize.1 = (f32[1024,1024]{1,0:T(8,128)}, f32[64,1024]{1,0:T(8,128)S(1)}, f32[64,1024]{1,0:T(8,128)S(1)}) custom-call(f32[1536,512]{1,0:T(8,128)S(1)} %bitcast.25, f32[64,1024]{1,0:T(8,128)S(1)} %copy-done.1), custom_call_target="tpu_custom_call" | custom-call | flops 80000000000 | bytes 12000000 | tf_op jit(solution)/shard_map/factorize/pallas_call | solution.py:181
  262.2 0.7 copy-done.2
  262.9 1.8 constant_dynamic-slice_fusion
  264.8 1.3 copy.21
  266.1 7.9 %fusion = f32[64,64,16]{1,0,2:T(8,128)S(1)} fusion(f32[8,16,8,1024]{3,2,1,0:T(8,128)} %bitcast.39, f32[64,1024]{1,0:T(8,128)} %copy-done.2), kind=kOutput, calls=%fused_computation | convolution fusion | flops 805306368 | bytes 4718592 | tf_op jit(solution)/shard_map/rk,ink->rin/dot_general | solution.py:223
  274.1 0.3 copy.19
  274.4 0.2 copy.20
  274.5 1.0 fusion.3
  275.5 1.0 copy.22
  (19 shorter events, 0.2 us)
Async XLA Ops:
  7.2 0.7 copy-start.3
  7.9 0.7 copy-start.5
  15.7 7.6 %copy-start.6 = (s32[1,6]{1,0:T(1,128)S(1)}, s32[1,6]{1,0:T(1,128)}, u32[]{:S(2)}) copy-start(s32[1,6]{1,0:T(1,128)} %param.6) | copy-start | bytes 76
  15.7 63.3 %copy-start.4 = (f32[2048]{0:T(1024)S(1)}, f32[2048]{0:T(1024)}, u32[]{:S(2)}) copy-start(f32[2048]{0:T(1024)} %param.7) | copy-start | bytes 24580
  15.7 63.3 %all-to-all-start = ((f32[16,48,768]{2,1,0:T(8,128)}), f32[16,48,768]{2,1,0:T(8,128)S(1)}, u32[]{:S(2)}, u32[]{:S(2)}) async-start(f32[16,48,768]{2,1,0:T(8,128)} %gram.1), calls=%async_computation | async-start | bytes 4718592 | tf_op jit(solution)/shard_map/all_to_all | solution.py:212
  23.3 112.6 %all-gather.6.cloned.1.call-start = ((), (), s32[]{:S(2)}) async-start(), calls=%async_computation.1 | async-start | bytes 3342336 | tf_op jit(solution)/shard_map/all_gather | solution.py:216
  81.2 54.7 %copy-start = (f32[16,8,2048]{2,1,0:T(8,128)}, f32[16,8,2048]{2,1,0:T(8,128)S(1)}, u32[]{:S(2)}) copy-start(f32[16,8,2048]{2,1,0:T(8,128)S(1)} %sum_pieces.1) | copy-start | bytes 3145732
  82.0 184.1 %all-gather.8.cloned.1.call-start = ((), (), s32[]{:S(2)}) async-start(), calls=%async_computation.2 | async-start | bytes 4456448 | tf_op jit(solution)/shard_map/all_gather | solution.py:218
  135.9 4.1 %copy-start.1 = (f32[64,1024]{1,0:T(8,128)S(1)}, f32[64,1024]{1,0:T(8,128)}, u32[]{:S(2)}) copy-start(f32[64,1024]{1,0:T(8,128)} %slice.16.own) | copy-start | bytes 786436
  262.2 0.7 copy-start.2
Sparse Core Ops, SparseCore 0:
  82.2 53.6 all-gather.5
  140.2 49.0 all-gather.7

commit v2 on v1

--- a/solution.py
+++ b/solution.py
@@ -8,6 +8,7 @@
 from jax.sharding import PartitionSpec as P
 
 BW = 128
+WIDTH = 8
 HI = lax.Precision.HIGHEST
 
 
@@ -92,34 +93,39 @@
     )(listed.reshape(-1), device.reshape(1), pieces, diag[None, :])
 
 
-def eliminate(tile):
+def eliminate(tile, width=WIDTH):
     tiles = BW // 8
     sub = lax.broadcasted_iota(jnp.int32, (8, BW), 0)
     lane = lax.broadcasted_iota(jnp.int32, (8, BW), 1)
     a = [tile[8 * g : 8 * g + 8, :] for g in range(tiles)]
     v = [jnp.where(lane == sub + 8 * g, 1.0, 0.0).astype(jnp.float32) for g in range(tiles)]
-    for j in range(0, BW, 2):
+    for j in range(0, BW, width):
         g0, s0 = j // 8, j % 8
-        row0, row1 = a[g0][s0 : s0 + 1, :], a[g0][s0 + 1 : s0 + 2, :]
-        inv0, inv1 = v[g0][s0 : s0 + 1, :], v[g0][s0 + 1 : s0 + 2, :]
-        pivot = row0[:, j : j + 1]
-        cross = row0[:, j + 1 : j + 2]
-        other = row1[:, j + 1 : j + 2]
-        recip = 1.0 / pivot
-        ratio = cross * recip
-        recip1 = 1.0 / (other - cross * ratio)
-        next_row = row1 - ratio * row0
-        next_inv = inv1 - ratio * inv0
-        row0s, inv0s = row0 * recip, inv0 * recip
-        row1s, inv1s = next_row * recip1, next_inv * recip1
+        rows = [jnp.broadcast_to(a[g0][s0 + t : s0 + t + 1, :], (8, BW)) for t in range(width)]
+        invs = [jnp.broadcast_to(v[g0][s0 + t : s0 + t + 1, :], (8, BW)) for t in range(width)]
+        core = [
+            [jnp.broadcast_to(rows[t][:, j + u : j + u + 1], (8, BW)) for u in range(width)] for t in range(width)
+        ]
+        ratios = []
+        for t in range(width):
+            recip = 1.0 / core[t][t]
+            ratio = [core[t][u] * recip for u in range(width)]
+            for u in range(t + 1, width):
+                for w in range(u, width):
+                    core[u][w] = core[u][w] - ratio[u] * core[t][w]
+                rows[u] = rows[u] - ratio[u] * rows[t]
+                invs[u] = invs[u] - ratio[u] * invs[t]
+            ratios.append(ratio)
+            rows[t], invs[t] = rows[t] * recip, invs[t] * recip
         for g in range(g0, tiles):
-            c0 = jnp.broadcast_to(a[g][:, j : j + 1], (8, BW))
-            c1 = jnp.broadcast_to(a[g][:, j + 1 : j + 2], (8, BW)) - c0 * ratio
-            if g == g0:
-                c0 = jnp.where(sub > s0, c0, 0.0)
-                c1 = jnp.where(sub > s0 + 1, c1, 0.0)
-            a[g] = a[g] - c0 * row0s - c1 * row1s
-            v[g] = v[g] - c0 * inv0s - c1 * inv1s
+            own = [jnp.broadcast_to(a[g][:, j + t : j + t + 1], (8, BW)) for t in range(width)]
+            for t in range(width):
+                for u in range(t + 1, width):
+                    own[u] = own[u] - own[t] * ratios[t][u]
+            for t in range(width):
+                use = jnp.where(sub > s0 + t, own[t], 0.0) if g == g0 else own[t]
+                a[g] = a[g] - use * rows[t]
+                v[g] = v[g] - use * invs[t]
     upper, inverse = [], []
     for g in range(tiles):
         own = jnp.sum(jnp.where(lane == sub + 8 * g, a[g], 0.0), axis=1, keepdims=True)

time: 284 us -> 214 us (0.75)
  Pallas kernels: 131 us -> 61.8 us
    pallas_call x1, Pallas kernels: 122 us -> 52.4 us  [factorize(): pl.pallas_call(factor_kernel, out_shape=(jax.ShapeDtypeStruct((panel, pan...]
  transfers between devices with their start and end apart: 3 -> 3, of which waited for: 1 -> 1; matrix products, arithmetic and copies ran while one was open for 2% -> 2% of each run, Pallas kernels for 43% -> 25%
where the time goes in v2:
time: 214 us
  Pallas kernels  61.8 us (29%)
  blocking collectives  54.5 us (25%)
  waiting for transfers between devices  53.1 us (25%)
  between operations  14.2 us (7%)
  local copies, waits for them, and re-layouts  12.1 us (6%)
  matrix products  7.94 us (4%)
  starting transfers between devices  7.59 us (4%)
  other arithmetic  2.46 us (1%)
    all_gather x1, blocking collectives, shards(): all_listed = lax.all_gather(listed, 'scen')  54.5 us
    all_gather x1, waiting for transfers between devices, shards(): top = lax.all_gather(head[:, None, :], 'scen', axis=1, tiled=True)  53.1 us
    pallas_call x1, Pallas kernels, factorize(): pl.pallas_call(factor_kernel, out_shape=(jax.ShapeDtypeStruct((panel, pan...  52.4 us
    unnamed x18, local copies, waits for them, and re-layouts  8.53 us
    dot_general x1, matrix products, shards(): update = jnp.einsum('rk,ink->rin', solved, bottom, precision=HI)  7.94 us
    all_to_all x1, starting transfers between devices, shards(): pieces = lax.all_to_all(pieces, 'scen', 0, 0)  7.51 us
    pallas_call x1, Pallas kernels, gram(): pl.pallas_call(functools.partial(gram_kernel, touched=touched, count=coun...  7.22 us
  transfers between devices with their start and end apart: 3, of which 1 were waited for; matrix products, arithmetic and copies ran while one was open for 2% of the time, Pallas kernels for 25%

profile of v2, /device:TPU:0, one launch (start us, length us, event | category | flops | bytes accessed | tf_op | source)
XLA Modules:
  0.0 213.7 jit_solution(9033727068589679962)
XLA Ops:
  7.2 0.7 copy-done.3
  7.9 0.7 copy-done.5
  8.5 7.2 %gram.1 = f32[16,48,768]{2,1,0:T(8,128)} custom-call(s32[6]{0:T(128)S(1)} %bitcast.31, bf16[2048,2048]{1,0:T(8,128)(2,1)} %bitcast.33, bf16[2048,2048]{1,0:T(8,128)(2,1)} %bitcast.34, bf16[2048,2048]{1,0:T(8,128)(2,1)} %bitcast.35, bf16[2048,2048]{1,0:T(8,128)(2,1)} %bitcast.36, bf16[2048,2048]{1,0:T(8,128)(2,1)} %bitcast.37, bf16[2048,2048]{1,0:T(8,128)(2,1)} %bitcast.38, ...), custom_call_target="tpu_custom_call" | custom-call | tf_op jit(solution)/shard_map/gram/pallas_call | solution.py:43
  15.7 7.5 %all-to-all-start = ((f32[16,48,768]{2,1,0:T(8,128)}), f32[16,48,768]{2,1,0:T(8,128)S(1)}, u32[]{:S(2)}, u32[]{:S(2)}) async-start(f32[16,48,768]{2,1,0:T(8,128)} %gram.1), calls=%async_computation | async-start | bytes 4718592 | tf_op jit(solution)/shard_map/all_to_all | solution.py:218
  23.3 0.0 all-gather.6.cloned.1.call-start
  23.3 54.5 %all-gather.2 = s32[16,1,6]{2,1,0:T(1,128)S(1)} all-gather(s32[1,1,6]{2,1,0:T(1,128)S(1)} %bitcast.32), channel_id=1, replica_groups=mesh['group'=2,'scen'=16] {'scen'}, dimensions={0}, use_global_device_ids=true | all-gather | bytes 408 | tf_op jit(solution)/shard_map/all_gather | solution.py:216
  77.8 0.5 broadcast.3
  78.3 0.7 reduce.3
  79.0 0.1 reshape.22.listed
  79.1 2.1 sum_pieces.1
  81.3 0.8 pad_maximum_fusion
  82.0 0.0 all-gather.8.cloned.1.call-start
  82.1 0.7 slice.16.own
  82.8 53.1 %all-gather.6.cloned.1.call-done = f32[96,8192]{1,0:T(8,128)} async-done(((f32[96,512]{1,0:T(8,128)}), f32[96,8192]{1,0:T(8,128)}) %all-gather.6.cloned.1.call-update) | async-done | bytes 3145744 | tf_op jit(solution)/shard_map/all_gather | solution.py:222
  135.9 4.1 %copy.25 = f32[12,8,16,512]{3,2,1,0:T(8,128)S(1)} copy(f32[12,8,16,512]{3,1,2,0:T(8,128)} %bitcast.40) | data formatting | bytes 6291456
  140.1 52.4 %factorize.1 = (f32[1024,1024]{1,0:T(8,128)}, f32[64,1024]{1,0:T(8,128)S(1)}, f32[64,1024]{1,0:T(8,128)S(1)}) custom-call(f32[1536,512]{1,0:T(8,128)S(1)} %bitcast.25, f32[64,1024]{1,0:T(8,128)S(1)} %copy-done.1), custom_call_target="tpu_custom_call" | custom-call | flops 80000000000 | bytes 12000000 | tf_op jit(solution)/shard_map/factorize/pallas_call | solution.py:187
  192.5 0.7 copy-done.2
  193.2 1.8 constant_dynamic-slice_fusion
  195.1 1.3 copy.21
  196.4 7.9 %fusion = f32[64,64,16]{1,0,2:T(8,128)S(1)} fusion(f32[8,16,8,1024]{3,2,1,0:T(8,128)} %bitcast.39, f32[64,1024]{1,0:T(8,128)} %copy-done.2), kind=kOutput, calls=%fused_computation | convolution fusion | flops 805306368 | bytes 4718592 | tf_op jit(solution)/shard_map/rk,ink->rin/dot_general | solution.py:229
  204.4 0.3 copy.19
  204.7 0.2 copy.20
  204.9 1.0 fusion.3
  205.9 1.0 copy.22
  (19 shorter events, 0.2 us)
Async XLA Ops:
  7.2 0.7 copy-start.3
  7.9 0.7 copy-start.5
  15.7 7.6 %copy-start.6 = (s32[1,6]{1,0:T(1,128)S(1)}, s32[1,6]{1,0:T(1,128)}, u32[]{:S(2)}) copy-start(s32[1,6]{1,0:T(1,128)} %param.6) | copy-start | bytes 76
  15.7 63.3 %copy-start.4 = (f32[2048]{0:T(1024)S(1)}, f32[2048]{0:T(1024)}, u32[]{:S(2)}) copy-start(f32[2048]{0:T(1024)} %param.7) | copy-start | bytes 24580
  15.7 63.3 %all-to-all-start = ((f32[16,48,768]{2,1,0:T(8,128)}), f32[16,48,768]{2,1,0:T(8,128)S(1)}, u32[]{:S(2)}, u32[]{:S(2)}) async-start(f32[16,48,768]{2,1,0:T(8,128)} %gram.1), calls=%async_computation | async-start | bytes 4718592 | tf_op jit(solution)/shard_map/all_to_all | solution.py:218
  23.3 112.6 %all-gather.6.cloned.1.call-start = ((), (), s32[]{:S(2)}) async-start(), calls=%async_computation.1 | async-start | bytes 3342336 | tf_op jit(solution)/shard_map/all_gather | solution.py:222
  81.2 54.7 %copy-start = (f32[16,8,2048]{2,1,0:T(8,128)}, f32[16,8,2048]{2,1,0:T(8,128)S(1)}, u32[]{:S(2)}) copy-start(f32[16,8,2048]{2,1,0:T(8,128)S(1)} %sum_pieces.1) | copy-start | bytes 3145732
  82.0 114.4 %all-gather.8.cloned.1.call-start = ((), (), s32[]{:S(2)}) async-start(), calls=%async_computation.2 | async-start | bytes 4456448 | tf_op jit(solution)/shard_map/all_gather | solution.py:224
  135.9 4.1 %copy-start.1 = (f32[64,1024]{1,0:T(8,128)S(1)}, f32[64,1024]{1,0:T(8,128)}, u32[]{:S(2)}) copy-start(f32[64,1024]{1,0:T(8,128)} %slice.16.own) | copy-start | bytes 786436
  192.5 0.7 copy-start.2
Sparse Core Ops, SparseCore 0:
  82.2 53.6 all-gather.5
  140.2 48.7 all-gather.7
